TPU v7x, 32 devices: a whole 2x2x4 slice. The times are simulated.
32 devices in a mesh: seg: 2 (over y), ch: 16 (over z, x, core).
Axes of the slice: x: 2, y: 2, z: 4, core: 2. Of those that a mesh axis runs over, the one named last changes fastest.
Arguments:
- strain: float32 [2, 1024, 2048], P('seg', 'ch')
- ref_local: int32 [4, 16], replicated, may hold values from 0 to 127, as said below
- owners: int32 [4], replicated, may hold values from 0 to 15, as said below
Outputs:
- toeplitz_blocks: float32 [64, 2048, 64], P('seg', 'ch')
Inputs may be any that keep to these rules, and one draw needn't show every extreme that they name: `ref_local`: each row holds 16 distinct offsets; the first row holds 127. `owners`: the 4 entries are distinct, and one of them is 15.
All inputs are finite; a program needn't handle non-finite values.
Results may differ from a plain program's by a relative error of at most 0.0029.
Values may be sent and summed in bfloat16 or wider, within the bound.
A program may use at most 64 MiB of HBM per device.

v0:
```python
import jax
import jax.numpy as jnp
from jax import lax
from jax.sharding import PartitionSpec as P

L = 64


def spread_2(block, axis, holder):
    block = jnp.where(lax.axis_index(axis) == holder, block, jnp.zeros_like(block))
    return lax.psum(block, axis)


def detrend_cols(series):
    n_total = series.shape[0]
    mid_time = (n_total - 1) / 2.0
    spread = n_total * (n_total * n_total - 1) / 12.0
    centred = (jnp.arange(n_total, dtype=jnp.float32) - mid_time)[:, None]
    level_val = jnp.sum(series, axis=0) / n_total
    slope_val = jnp.sum(centred * series, axis=0) / spread
    return (series - level_val - slope_val * centred).astype(jnp.bfloat16)


def owner_panels(detrended, ref_local, owners):
    pieces = []
    for panel_id in range(ref_local.shape[0]):
        own_cols = jnp.take(detrended, ref_local[panel_id], axis=1)
        pieces.append(spread_2(own_cols, "ch", owners[panel_id]))
    return jnp.concatenate(pieces, axis=1)


def per_device(strain, ref_local, owners):
    my_rows = strain[0]
    s_dev, chans = my_rows.shape
    n_ch = lax.axis_size("ch")
    n_seg = lax.axis_size("seg")
    n_total = s_dev * n_ch
    c_dev = chans // n_ch
    series = lax.all_to_all(my_rows, "ch", split_axis=1, concat_axis=0, tiled=True)
    detrended = detrend_cols(series)
    panels = owner_panels(detrended, ref_local, owners)
    width_ref = panels.shape[1]
    padded = jnp.concatenate([detrended, jnp.zeros((L, c_dev), jnp.bfloat16)], axis=0)
    blk_rows = min(512, n_total)
    n_blocks = n_total // blk_rows
    lag_dev = L // n_seg
    lag_count = lax.axis_size("seg") * lag_dev

    def add_block(blk_idx, running):
        blk_start = blk_idx * blk_rows
        window = lax.dynamic_slice_in_dim(padded, blk_start, blk_rows + lag_count - 1, 0)
        lagged = jnp.concatenate(
            [window[lag_off : lag_off + blk_rows] for lag_off in range(lag_count)], axis=1
        )
        ref_block = lax.dynamic_slice_in_dim(panels, blk_start, blk_rows, 0)
        return running + lax.dot_general(
            lagged, ref_block, (((0,), (0,)), ((), ())), preferred_element_type=jnp.float32
        )

    start_acc = jnp.zeros((lag_count * c_dev, width_ref), jnp.float32)
    running = lax.fori_loop(0, n_blocks, add_block, start_acc)
    summed = lax.psum_scatter(
        running.reshape(lag_count, c_dev, width_ref), "seg", scatter_dimension=0, tiled=True
    )
    lag_ids = (lax.axis_index("seg") * lag_dev + jnp.arange(lag_dev, dtype=jnp.int32)).astype(
        jnp.float32
    )
    return summed / (n_seg * (n_total - lag_ids))[:, None, None]


def solution(mesh):
    in_specs = (P("seg", "ch", None), P(), P())
    out_specs = P("seg", "ch", None)
    return jax.shard_map(
        per_device, mesh=mesh, in_specs=in_specs, out_specs=out_specs, check_vma=False
    )
```

profile of v0, /device:TPU:0, one launch (start us, length us, event | category | flops | bytes accessed | tf_op | source)
XLA Modules:
  0.0 272.1 jit_solution(4993539267196957720)
XLA Ops:
  6.5 1.1 copy.23
  7.7 1.0 copy.16
  8.6 7.4 %all-to-all-start = ((f32[64,16,128]{2,0,1:T(8,128)}), f32[64,16,128]{2,0,1:T(8,128)S(1)}, u32[]{:S(2)}, u32[]{:S(2)}) async-start(f32[64,16,128]{2,0,1:T(8,128)} %copy.16), calls=%async_computation | async-start | bytes 1048576 | tf_op jit(solution)/shard_map/all_to_all | solution.py:39
  16.1 1.5 fusion.3
  20.0 0.8 compare_and_fusion.3
  20.9 9.4 %all-to-all-done = f32[64,16,128]{2,0,1:T(8,128)S(1)} async-done(((f32[64,16,128]{2,0,1:T(8,128)}), f32[64,16,128]{2,0,1:T(8,128)S(1)}, u32[]{:S(2)}, u32[]{:S(2)}) %all-to-all-start) | async-done | bytes 524320 | tf_op jit(solution)/shard_map/all_to_all | solution.py:39
  36.4 88.2 %all-reduce.4.cloned.1.call-done = (bf16[1024,16]{0,1:T(8,128)(2,1)}, bf16[1024,16]{0,1:T(8,128)(2,1)}, bf16[1024,16]{0,1:T(8,128)(2,1)}, bf16[1024,16]{0,1:T(8,128)(2,1)}) async-done(((bf16[1024,16]{0,1:T(8,128)(2,1)}, bf16[1024,16]{0,1:T(8,128)(2,1)}, bf16[1024,16]{0,1:T(8,128)(2,1)}, bf16[1024,16]{0,1:T(8,128)(2,1)}), (bf16[1024,16]{0,1:T(8,128)(2,1)}, bf16[1024,16]{0,1:T(8,128)(2,1)}, ...) | async-done | bytes 131088 | tf_op jit(solution)/shard_map/psum | solution.py:11
  124.6 0.8 pad_maximum_fusion
  125.4 101.3 %while.14 = (s32[]{:T(128)}, f32[8192,64]{0,1:T(8,128)S(1)}, bf16[1088,128]{1,0:T(8,128)(2,1)S(1)}, bf16[1024,64]{0,1:T(8,128)(2,1)S(1)}, s32[]{:T(128)}, /*inde...) while((s32[]{:T(128)}, f32[8192,64]{0,1:T(8,128)S(1)}, ...), condition=%wide.region_7.9_spmd.clone, body=%wide.region_6.8_spmd.clone.sunk | while | flops 537919552 | bytes 29427356 | solution.py:61
  135.3 0.8 constant_dynamic-update-slice_fusion.142
  143.1 0.7 constant_dynamic-update-slice_fusion.153
  146.7 0.8 constant_dynamic-update-slice_fusion.158
  150.3 0.8 constant_dynamic-update-slice_fusion.163
  163.1 0.8 constant_dynamic-update-slice_fusion.181
  170.9 5.2 %convolution_add_fusion.2 = f32[8192,64]{0,1:T(8,128)S(1)} fusion(bf16[512,8192]{1,0:T(8,128)(2,1)} %constant_dynamic-update-slice_fusion.191, f32[8192,64]{0,1:T(8,128)S(1)} %get-tuple-element.251, pred[]{:T(512)S(6)} %compare.4, bf16[1024,64]{0,1:T(8,128)(2,1)S(1)} %get-tuple-element.325, s32[]{:T(128)S(6)} %select_n.98), kind=kOutput, calls=%fused_computation.4.clone.1 | convolution fusion | flops 537919488 | bytes 12648453 | tf_op jit(solution)/shard_map/while/body/eval_jaxpr/dot_general | solution.py:56
  185.9 0.8 constant_dynamic-update-slice_fusion.142
  197.3 0.8 constant_dynamic-update-slice_fusion.158
  200.9 0.8 constant_dynamic-update-slice_fusion.163
  213.7 0.8 constant_dynamic-update-slice_fusion.181
  221.5 5.2 %convolution_add_fusion.2 = f32[8192,64]{0,1:T(8,128)S(1)} fusion(bf16[512,8192]{1,0:T(8,128)(2,1)} %constant_dynamic-update-slice_fusion.191, f32[8192,64]{0,1:T(8,128)S(1)} %get-tuple-element.251, pred[]{:T(512)S(6)} %compare.4, bf16[1024,64]{0,1:T(8,128)(2,1)S(1)} %get-tuple-element.325, s32[]{:T(128)S(6)} %select_n.98), kind=kOutput, calls=%fused_computation.4.clone.1 | convolution fusion | flops 537919488 | bytes 12648453 | tf_op jit(solution)/shard_map/while/body/eval_jaxpr/dot_general | solution.py:56
  226.7 1.7 copy.24
  228.5 33.8 %reduce-scatter.2.cloned.1.call-done = f32[32,128,64]{1,0,2:T(8,128)} async-done(((f32[64,128,64]{1,0,2:T(8,128)}), f32[32,128,64]{1,0,2:T(8,128)}) %reduce-scatter.2.cloned.1.call-update) | async-done | bytes 1048592 | tf_op jit(solution)/shard_map/reduce_scatter | solution.py:62
  262.3 1.4 broadcast_divide_fusion
  263.7 1.6 copy.20
  (144 shorter events, 90.2 us)
Async XLA Ops:
  8.6 21.7 %all-to-all-start = ((f32[64,16,128]{2,0,1:T(8,128)}), f32[64,16,128]{2,0,1:T(8,128)S(1)}, u32[]{:S(2)}, u32[]{:S(2)}) async-start(f32[64,16,128]{2,0,1:T(8,128)} %copy.16), calls=%async_computation | async-start | bytes 1048576 | tf_op jit(solution)/shard_map/all_to_all | solution.py:39
  16.0 108.6 %all-reduce.4.cloned.1.call-start = ((), (), s32[]{:S(2)}) async-start(), calls=%async_computation.3 | async-start | bytes 262144 | tf_op jit(solution)/shard_map/psum | solution.py:11
  36.2 226.1 %reduce-scatter.2.cloned.1.call-start = ((), (), s32[]{:S(2)}) async-start(), calls=%async_computation.2 | async-start | bytes 3145728 | tf_op jit(solution)/shard_map/reduce_scatter | solution.py:62
Sparse Core Ops, SparseCore 0:
  36.3 88.2 all-reduce.3
  228.6 33.6 reduce-scatter.1
where the time goes:
time: 273 us; the launch traced here: 272 us
  waiting for transfers between devices  131 us (48%)
  local copies, waits for them, and re-layouts  100 us (37%)
  between operations  16 us (6%)
  matrix products  10.4 us (4%)
  starting transfers between devices  7.47 us (3%)
  other arithmetic  6.38 us (2%)
    while x126, local copies, waits for them, and re-layouts  89.4 us
    psum x1, waiting for transfers between devices, spread_2(): return lax.psum(block, axis)  88.2 us
    reduce_scatter x1, waiting for transfers between devices, per_device(): lax.psum_scatter(running.reshape(lag_count, c_dev, width_ref), 'seg', sca...  33.8 us
    dot_general x2, matrix products, add_block(): lax.dot_general(lagged, ref_block, (((0,), (0,)), ((), ())), preferred_el...  10.4 us
    all_to_all x1, waiting for transfers between devices, per_device(): lax.all_to_all(my_rows, 'ch', split_axis=1, concat_axis=0, tiled=True)  9.4 us
    all_to_all x1, starting transfers between devices, per_device(): lax.all_to_all(my_rows, 'ch', split_axis=1, concat_axis=0, tiled=True)  7.39 us
  transfers between devices with their start and end apart: 3, of which 3 were waited for; matrix products, arithmetic and copies ran while one was open for 1% of the time, Pallas kernels for 0%

commit v1 on v0

--- a/solution.py
+++ b/solution.py
@@ -4,6 +4,30 @@
 from jax.sharding import PartitionSpec as P
 
 L = 64
+
+
+def split_up(x, dim, count):
+    shape = x.shape
+    blocks = x.reshape(*shape[:dim], count, shape[dim] // count, *shape[dim + 1 :])
+    return jnp.moveaxis(blocks, dim, 0)
+
+
+def joined_along(tiles, dim):
+    tiles = jnp.moveaxis(tiles, 0, dim)
+    dims = tiles.shape
+    return tiles.reshape(*dims[:dim], dims[dim] * dims[dim + 1], *dims[dim + 2 :])
+
+
+def sent_to_each(x, axis, split_dim, concat_dim):
+    size, place = (lax.axis_size(axis), lax.axis_index(axis))
+    blocks = split_up(x, split_dim, size)
+    out = blocks
+    for step in range(1, size):
+        target, source = ((place + step) % size, (place - step) % size)
+        sent = lax.dynamic_index_in_dim(blocks, target, 0)
+        received = lax.ppermute(sent, axis, [(i, (i + step) % size) for i in range(size)])
+        out = lax.dynamic_update_slice_in_dim(out, received, source, axis=0)
+    return joined_along(out, concat_dim)
 
 
 def spread_2(block, axis, holder):
@@ -36,7 +60,7 @@
     n_seg = lax.axis_size("seg")
     n_total = s_dev * n_ch
     c_dev = chans // n_ch
-    series = lax.all_to_all(my_rows, "ch", split_axis=1, concat_axis=0, tiled=True)
+    series = sent_to_each(my_rows, "ch", 1, 0)
     detrended = detrend_cols(series)
     panels = owner_panels(detrended, ref_local, owners)
     width_ref = panels.shape[1]

time: 273 us -> 281 us (1.029)
  starting transfers between devices: 7.47 us -> 24.5 us
  waiting for transfers between devices: 131 us -> 120 us
    ppermute x0 -> x15, starting transfers between devices: none -> 24.3 us  [sent_to_each(): lax.ppermute(sent, axis, [(i, (i + step) % size) for i in range(size)])]
    all_to_all x1 -> x0, waiting for transfers between devices: 9.4 us -> none  [per_device(): lax.all_to_all(my_rows, 'ch', split_axis=1, concat_axis=0, tiled=True)]
    all_to_all x1 -> x0, starting transfers between devices: 7.39 us -> none  [per_device(): lax.all_to_all(my_rows, 'ch', split_axis=1, concat_axis=0, tiled=True)]
  transfers between devices with their start and end apart: 3 -> 17, of which waited for: 3 -> 2; matrix products, arithmetic and copies ran while one was open for 1% -> 2% of each run, Pallas kernels for 0% -> 0%
where the time goes in v1:
time: 281 us; the launch traced here: 280 us
  waiting for transfers between devices  120 us (43%)
  local copies, waits for them, and re-layouts  102 us (36%)
  starting transfers between devices  24.5 us (9%)
  between operations  16.3 us (6%)
  matrix products  10.4 us (4%)
  other arithmetic  6.2 us (2%)
    while x126, local copies, waits for them, and re-layouts  89.3 us
    psum x1, waiting for transfers between devices, spread_2(): return lax.psum(block, axis)  86.4 us
    reduce_scatter x1, waiting for transfers between devices, per_device(): lax.psum_scatter(running.reshape(lag_count, c_dev, width_ref), 'seg', sca...  33.8 us
    ppermute x15, starting transfers between devices, sent_to_each(): lax.ppermute(sent, axis, [(i, (i + step) % size) for i in range(size)])  24.3 us
    dot_general x2, matrix products, add_block(): lax.dot_general(lagged, ref_block, (((0,), (0,)), ((), ())), preferred_el...  10.4 us
  transfers between devices with their start and end apart: 17, of which 2 were waited for; matrix products, arithmetic and copies ran while one was open for 2% of the time, Pallas kernels for 0%

profile of v1, /device:TPU:0, one launch (start us, length us, event | category | flops | bytes accessed | tf_op | source)
XLA Modules:
  0.0 280.1 jit_solution(16589553328245704945)
XLA Ops:
  6.5 1.1 copy.33
  8.8 2.5 collective-permute-start.1
  11.3 2.4 collective-permute-start.2
  13.7 1.6 collective-permute-start.3
  15.5 0.8 compare_and_fusion.3
  16.4 1.5 fusion.3
  17.9 1.3 collective-permute-start.5
  19.1 4.3 %collective-permute-start.6 = (f32[1,64,128]{2,0,1:T(1,128)S(1)}, f32[1,64,128]{2,0,1:T(1,128)S(1)}, u32[]{:S(2)}, u32[]{:S(2)}) collective-permute-start(f32[1,64,128]{2,0,1:T(1,128)S(1)} %get-tuple-element.143), channel_id=1, source_target_pairs={{0,7},{1,8},{2,9},{3,10},{4,11},{5,12},{6,13},{7,14},{8,15},{9,0},... | collective-permute-start | bytes 98312 | tf_op jit(solution)/shard_map/ppermute | solution.py:28
  24.1 2.4 collective-permute-start.9
  26.5 2.9 %collective-permute-start.10 = (f32[1,64,128]{2,0,1:T(1,128)S(1)}, f32[1,64,128]{2,0,1:T(1,128)S(1)}, u32[]{:S(2)}, u32[]{:S(2)}) collective-permute-start(f32[1,64,128]{2,0,1:T(1,128)S(1)} %get-tuple-element.139), channel_id=1, source_target_pairs={{0,11},{1,12},{2,13},{3,14},{4,15},{5,0},{6,1},{7,2},{8,3},{9,4},{... | collective-permute-start | bytes 98312 | tf_op jit(solution)/shard_map/ppermute | solution.py:28
  29.4 1.8 collective-permute-start.11
  31.2 1.5 collective-permute-start.13
  32.7 2.2 collective-permute-start.14
  46.2 86.4 %all-reduce.4.cloned.1.call-done = (bf16[1024,16]{0,1:T(8,128)(2,1)}, bf16[1024,16]{0,1:T(8,128)(2,1)}, bf16[1024,16]{0,1:T(8,128)(2,1)}, bf16[1024,16]{0,1:T(8,128)(2,1)}) async-done(((bf16[1024,16]{0,1:T(8,128)(2,1)}, bf16[1024,16]{0,1:T(8,128)(2,1)}, bf16[1024,16]{0,1:T(8,128)(2,1)}, bf16[1024,16]{0,1:T(8,128)(2,1)}), (bf16[1024,16]{0,1:T(8,128)(2,1)}, bf16[1024,16]{0,1:T(8,128)(2,1)}, ...) | async-done | bytes 131088 | tf_op jit(solution)/shard_map/psum | solution.py:35
  132.6 0.8 pad_maximum_fusion
  133.4 101.3 %while.14 = (s32[]{:T(128)}, f32[8192,64]{0,1:T(8,128)S(1)}, bf16[1088,128]{1,0:T(8,128)(2,1)S(1)}, bf16[1024,64]{0,1:T(8,128)(2,1)S(1)}, s32[]{:T(128)}, /*inde...) while((s32[]{:T(128)}, f32[8192,64]{0,1:T(8,128)S(1)}, ...), condition=%wide.region_7.9_spmd.clone, body=%wide.region_6.8_spmd.clone.sunk | while | flops 537919552 | bytes 29427356 | solution.py:85
  163.9 0.8 constant_dynamic-update-slice_fusion.171
  178.8 5.2 %convolution_add_fusion.2 = f32[8192,64]{0,1:T(8,128)S(1)} fusion(bf16[512,8192]{1,0:T(8,128)(2,1)} %constant_dynamic-update-slice_fusion.191, f32[8192,64]{0,1:T(8,128)S(1)} %get-tuple-element.264, pred[]{:T(512)S(6)} %compare.34, bf16[1024,64]{0,1:T(8,128)(2,1)S(1)} %get-tuple-element.338, s32[]{:T(128)S(6)} %select_n.372), kind=kOutput, calls=%fused_computation.4.clone.1 | convolution fusion | flops 537919488 | bytes 12648453 | tf_op jit(solution)/shard_map/while/body/eval_jaxpr/dot_general | solution.py:80
  214.5 0.8 constant_dynamic-update-slice_fusion.171
  229.5 5.2 %convolution_add_fusion.2 = f32[8192,64]{0,1:T(8,128)S(1)} fusion(bf16[512,8192]{1,0:T(8,128)(2,1)} %constant_dynamic-update-slice_fusion.191, f32[8192,64]{0,1:T(8,128)S(1)} %get-tuple-element.264, pred[]{:T(512)S(6)} %compare.34, bf16[1024,64]{0,1:T(8,128)(2,1)S(1)} %get-tuple-element.338, s32[]{:T(128)S(6)} %select_n.372), kind=kOutput, calls=%fused_computation.4.clone.1 | convolution fusion | flops 537919488 | bytes 12648453 | tf_op jit(solution)/shard_map/while/body/eval_jaxpr/dot_general | solution.py:80
  234.7 1.7 copy.34
  236.4 33.8 %reduce-scatter.2.cloned.1.call-done = f32[32,128,64]{1,0,2:T(8,128)} async-done(((f32[64,128,64]{1,0,2:T(8,128)}), f32[32,128,64]{1,0,2:T(8,128)}) %reduce-scatter.2.cloned.1.call-update) | async-done | bytes 1048592 | tf_op jit(solution)/shard_map/reduce_scatter | solution.py:86
  270.2 1.4 broadcast_divide_fusion
  271.7 1.6 copy.30
  (187 shorter events, 99.7 us)
Async XLA Ops:
  6.5 126.1 %all-reduce.4.cloned.1.call-start = ((), (), s32[]{:S(2)}) async-start(), calls=%async_computation.2 | async-start | bytes 262144 | tf_op jit(solution)/shard_map/psum | solution.py:35
  8.2 9.6 %collective-permute-start = (f32[1,64,128]{2,0,1:T(1,128)S(1)}, f32[1,64,128]{2,0,1:T(1,128)S(1)}, u32[]{:S(2)}, u32[]{:S(2)}) collective-permute-start(f32[1,64,128]{2,0,1:T(1,128)S(1)} %get-tuple-element.149), channel_id=1, source_target_pairs={{0,1},{1,2},{2,3},{3,4},{4,5},{5,6},{6,7},{7,8},{8,9},{9,10},{10,1... | collective-permute-start | bytes 98312 | tf_op jit(solution)/shard_map/ppermute | solution.py:28
  8.8 10.3 %collective-permute-start.1 = (f32[1,64,128]{2,0,1:T(1,128)S(1)}, f32[1,64,128]{2,0,1:T(1,128)S(1)}, u32[]{:S(2)}, u32[]{:S(2)}) collective-permute-start(f32[1,64,128]{2,0,1:T(1,128)S(1)} %get-tuple-element.148), channel_id=1, source_target_pairs={{0,2},{1,3},{2,4},{3,5},{4,6},{5,7},{6,8},{7,9},{8,10},{9,11},{10,... | collective-permute-start | bytes 98312 | tf_op jit(solution)/shard_map/ppermute | solution.py:28
  11.3 12.1 %collective-permute-start.2 = (f32[1,64,128]{2,0,1:T(1,128)S(1)}, f32[1,64,128]{2,0,1:T(1,128)S(1)}, u32[]{:S(2)}, u32[]{:S(2)}) collective-permute-start(f32[1,64,128]{2,0,1:T(1,128)S(1)} %get-tuple-element.147), channel_id=1, source_target_pairs={{0,3},{1,4},{2,5},{3,6},{4,7},{5,8},{6,9},{7,10},{8,11},{9,12},{10... | collective-permute-start | bytes 98312 | tf_op jit(solution)/shard_map/ppermute | solution.py:28
  13.7 10.0 %collective-permute-start.3 = (f32[1,64,128]{2,0,1:T(1,128)S(1)}, f32[1,64,128]{2,0,1:T(1,128)S(1)}, u32[]{:S(2)}, u32[]{:S(2)}) collective-permute-start(f32[1,64,128]{2,0,1:T(1,128)S(1)} %get-tuple-element.146), channel_id=1, source_target_pairs={{0,4},{1,5},{2,6},{3,7},{4,8},{5,9},{6,10},{7,11},{8,12},{9,13},{1... | collective-permute-start | bytes 98312 | tf_op jit(solution)/shard_map/ppermute | solution.py:28
  15.3 8.8 %collective-permute-start.4 = (f32[1,64,128]{2,0,1:T(1,128)S(1)}, f32[1,64,128]{2,0,1:T(1,128)S(1)}, u32[]{:S(2)}, u32[]{:S(2)}) collective-permute-start(f32[1,64,128]{2,0,1:T(1,128)S(1)} %get-tuple-element.145), channel_id=1, source_target_pairs={{0,5},{1,6},{2,7},{3,8},{4,9},{5,10},{6,11},{7,12},{8,13},{9,14},{... | collective-permute-start | bytes 98312 | tf_op jit(solution)/shard_map/ppermute | solution.py:28
  17.9 8.6 %collective-permute-start.5 = (f32[1,64,128]{2,0,1:T(1,128)S(1)}, f32[1,64,128]{2,0,1:T(1,128)S(1)}, u32[]{:S(2)}, u32[]{:S(2)}) collective-permute-start(f32[1,64,128]{2,0,1:T(1,128)S(1)} %get-tuple-element.144), channel_id=1, source_target_pairs={{0,6},{1,7},{2,8},{3,9},{4,10},{5,11},{6,12},{7,13},{8,14},{9,15},... | collective-permute-start | bytes 98312 | tf_op jit(solution)/shard_map/ppermute | solution.py:28
  19.1 10.3 %collective-permute-start.6 = (f32[1,64,128]{2,0,1:T(1,128)S(1)}, f32[1,64,128]{2,0,1:T(1,128)S(1)}, u32[]{:S(2)}, u32[]{:S(2)}) collective-permute-start(f32[1,64,128]{2,0,1:T(1,128)S(1)} %get-tuple-element.143), channel_id=1, source_target_pairs={{0,7},{1,8},{2,9},{3,10},{4,11},{5,12},{6,13},{7,14},{8,15},{9,0},... | collective-permute-start | bytes 98312 | tf_op jit(solution)/shard_map/ppermute | solution.py:28
  23.5 7.8 %collective-permute-start.7 = (f32[1,64,128]{2,0,1:T(1,128)S(1)}, f32[1,64,128]{2,0,1:T(1,128)S(1)}, u32[]{:S(2)}, u32[]{:S(2)}) collective-permute-start(f32[1,64,128]{2,0,1:T(1,128)S(1)} %get-tuple-element.142), channel_id=1, source_target_pairs={{0,8},{1,9},{2,10},{3,11},{4,12},{5,13},{6,14},{7,15},{8,0},{9,1},... | collective-permute-start | bytes 98312 | tf_op jit(solution)/shard_map/ppermute | solution.py:28
  23.8 7.4 %collective-permute-start.8 = (f32[1,64,128]{2,0,1:T(1,128)S(1)}, f32[1,64,128]{2,0,1:T(1,128)S(1)}, u32[]{:S(2)}, u32[]{:S(2)}) collective-permute-start(f32[1,64,128]{2,0,1:T(1,128)S(1)} %get-tuple-element.141), channel_id=1, source_target_pairs={{0,9},{1,10},{2,11},{3,12},{4,13},{5,14},{6,15},{7,0},{8,1},{9,2},... | collective-permute-start | bytes 98312 | tf_op jit(solution)/shard_map/ppermute | solution.py:28
  24.1 8.6 %collective-permute-start.9 = (f32[1,64,128]{2,0,1:T(1,128)S(1)}, f32[1,64,128]{2,0,1:T(1,128)S(1)}, u32[]{:S(2)}, u32[]{:S(2)}) collective-permute-start(f32[1,64,128]{2,0,1:T(1,128)S(1)} %get-tuple-element.140), channel_id=1, source_target_pairs={{0,10},{1,11},{2,12},{3,13},{4,14},{5,15},{6,0},{7,1},{8,2},{9,3},... | collective-permute-start | bytes 98312 | tf_op jit(solution)/shard_map/ppermute | solution.py:28
  26.5 12.6 %collective-permute-start.10 = (f32[1,64,128]{2,0,1:T(1,128)S(1)}, f32[1,64,128]{2,0,1:T(1,128)S(1)}, u32[]{:S(2)}, u32[]{:S(2)}) collective-permute-start(f32[1,64,128]{2,0,1:T(1,128)S(1)} %get-tuple-element.139), channel_id=1, source_target_pairs={{0,11},{1,12},{2,13},{3,14},{4,15},{5,0},{6,1},{7,2},{8,3},{9,4},{... | collective-permute-start | bytes 98312 | tf_op jit(solution)/shard_map/ppermute | solution.py:28
  29.4 9.8 %collective-permute-start.11 = (f32[1,64,128]{2,0,1:T(1,128)S(1)}, f32[1,64,128]{2,0,1:T(1,128)S(1)}, u32[]{:S(2)}, u32[]{:S(2)}) collective-permute-start(f32[1,64,128]{2,0,1:T(1,128)S(1)} %get-tuple-element.138), channel_id=1, source_target_pairs={{0,12},{1,13},{2,14},{3,15},{4,0},{5,1},{6,2},{7,3},{8,4},{9,5},{1... | collective-permute-start | bytes 98312 | tf_op jit(solution)/shard_map/ppermute | solution.py:28
  31.2 8.2 %collective-permute-start.12 = (f32[1,64,128]{2,0,1:T(1,128)S(1)}, f32[1,64,128]{2,0,1:T(1,128)S(1)}, u32[]{:S(2)}, u32[]{:S(2)}) collective-permute-start(f32[1,64,128]{2,0,1:T(1,128)S(1)} %get-tuple-element.137), channel_id=1, source_target_pairs={{0,13},{1,14},{2,15},{3,0},{4,1},{5,2},{6,3},{7,4},{8,5},{9,6},{10... | collective-permute-start | bytes 98312 | tf_op jit(solution)/shard_map/ppermute | solution.py:28
  31.2 8.3 %collective-permute-start.13 = (f32[1,64,128]{2,0,1:T(1,128)S(1)}, f32[1,64,128]{2,0,1:T(1,128)S(1)}, u32[]{:S(2)}, u32[]{:S(2)}) collective-permute-start(f32[1,64,128]{2,0,1:T(1,128)S(1)} %get-tuple-element.136), channel_id=1, source_target_pairs={{0,14},{1,15},{2,0},{3,1},{4,2},{5,3},{6,4},{7,5},{8,6},{9,7},{10,... | collective-permute-start | bytes 98312 | tf_op jit(solution)/shard_map/ppermute | solution.py:28
  32.7 7.0 %collective-permute-start.14 = (f32[1,64,128]{2,0,1:T(1,128)S(1)}, f32[1,64,128]{2,0,1:T(1,128)S(1)}, u32[]{:S(2)}, u32[]{:S(2)}) collective-permute-start(f32[1,64,128]{2,0,1:T(1,128)S(1)} %get-tuple-element.135), channel_id=1, source_target_pairs={{0,15},{1,0},{2,1},{3,2},{4,3},{5,4},{6,5},{7,6},{8,7},{9,8},{10,9... | collective-permute-start | bytes 98312 | tf_op jit(solution)/shard_map/ppermute | solution.py:28
  45.7 224.5 %reduce-scatter.2.cloned.1.call-start = ((), (), s32[]{:S(2)}) async-start(), calls=%async_computation.1 | async-start | bytes 3145728 | tf_op jit(solution)/shard_map/reduce_scatter | solution.py:86
Sparse Core Ops, SparseCore 0:
  45.9 86.6 all-reduce.3
  236.5 33.6 reduce-scatter.1
